TPU v7x, 32 devices: a whole 2x2x4 slice. The times are simulated.
32 devices in a mesh: region: 4 (over y, core), shard: 8 (over z, x).
Axes of the slice: x: 2, y: 2, z: 4, core: 2. Of those that a mesh axis runs over, the one named last changes fastest.
Arguments:
- fields: bfloat16 [32, 16384], P('shard', 'region'), may hold values from -6 to 6
- near_coef: bfloat16 [128, 3, 128, 128], P(('region', 'shard')), may hold values from -0.25 to 0.25
- far_coef: bfloat16 [128, 2, 128, 128], P(('region', 'shard')), may hold values from -0.25 to 0.25
- inv_factor: bfloat16 [128, 128, 128], P(('region', 'shard')), as said below
- near_block: int32 [128, 3], P(('region', 'shard')), may hold values from 0 to 3, as said below
- far_region: int32 [128, 2], P(('region', 'shard')), may hold values from 0 to 3, all different within a row; in each aligned block of 4 rows (0 to 3, 4 to 7, ...) at most 2 rows name the same one
- far_block: int32 [128, 2], P(('region', 'shard')), may hold values from 0 to 3
Outputs:
- whitened: bfloat16 [32, 16384], P('shard', 'region')
Inputs may be any that keep to these rules, and one draw needn't show every extreme that they name: inv_factor[g] is upper triangular with a positive diagonal. `near_block`: row g lists 3 different indices of its own group of 4 blocks, never g % 4 itself. `far_region`: each row names 2 different regions; within the rows of one group of 4 blocks no region is named more than 2 times.
All inputs are finite; a program needn't handle non-finite values.
Results may differ from a plain program's by a relative error of at most 0.0049.
Values may be sent and summed in bfloat16 or wider, within the bound.
A program may use at most 64 MiB of HBM per device.

v0:
```python
import jax
import jax.numpy as jnp
from jax import lax
from jax.sharding import PartitionSpec as P


def rank_within(regions):
    entries = regions.shape[-1]
    identical = regions[..., :, None] == regions[..., None, :]
    earlier = jnp.arange(entries)[None, :] < jnp.arange(entries)[:, None]
    return jnp.sum(jnp.logical_and(identical, earlier), axis=-1)


def slot_sources(regions, blocks, target, capacity):
    rank_list = rank_within(regions)
    wanted = jnp.logical_and(
        (regions == target)[..., :, None], rank_list[..., :, None] == jnp.arange(capacity)
    )
    return jnp.sum(jnp.where(wanted, blocks[..., :, None], 0), axis=-2)


def selector(indices, count):
    return (indices[..., None] == jnp.arange(count, dtype=jnp.int32)).astype(jnp.bfloat16)


def body(fields, near_coef, far_coef, inv_factor, near_block, far_region, far_block):
    samp_rows = fields.shape[0]
    shard_count = lax.axis_size("shard")
    region_count = lax.axis_size("region")
    blocks_here, far_count = far_region.shape
    block_width = near_coef.shape[-1]
    entries = blocks_here * far_count
    capacity = max(2, -(-entries // region_count))
    slot_count = region_count * capacity
    own_region = lax.axis_index("region")
    flat_regions = far_region.reshape(entries)
    own_slots = flat_regions * capacity + rank_within(flat_regions)
    wanted_regions, wanted_blocks = (
        lax.all_gather(far_region, ("region", "shard"), axis=0, tiled=True),
        lax.all_gather(far_block, ("region", "shard"), axis=0, tiled=True),
    )
    sources = slot_sources(
        wanted_regions.reshape(region_count, shard_count, entries),
        wanted_blocks.reshape(region_count, shard_count, entries),
        own_region,
        capacity,
    )
    sources = jnp.transpose(sources, (1, 0, 2)).reshape(shard_count, slot_count)
    pick_send = selector(sources, blocks_here)
    sample_view = fields.reshape(samp_rows, shard_count, blocks_here, block_width)
    outgoing = jnp.einsum(
        "sgbd,gcb->sgcd", sample_view, pick_send, preferred_element_type=jnp.float32
    ).astype(jnp.bfloat16)
    outgoing = outgoing.reshape(samp_rows, shard_count, slot_count * block_width)
    arrived = lax.all_to_all(outgoing, "region", split_axis=2, concat_axis=2, tiled=True)
    combined = jnp.concatenate(
        [fields.reshape(samp_rows, shard_count, blocks_here * block_width), arrived], axis=2
    )
    transposed = lax.all_to_all(combined, "shard", split_axis=1, concat_axis=0, tiled=True)
    total_rows = transposed.shape[0]
    block_data = transposed[:, 0, : blocks_here * block_width].reshape(
        total_rows, blocks_here, block_width
    )
    incoming = transposed[:, 0, blocks_here * block_width :].reshape(
        total_rows, slot_count, block_width
    )
    pick_far = selector(own_slots, slot_count)
    far_data = jnp.einsum(
        "scd,ec->sed", incoming, pick_far, preferred_element_type=jnp.float32
    ).astype(jnp.bfloat16)
    far_data = far_data.reshape(total_rows, blocks_here, far_count, block_width)
    pick_near = selector(near_block, blocks_here)
    near_data = jnp.einsum(
        "skd,bjk->sbjd", block_data, pick_near, preferred_element_type=jnp.float32
    ).astype(jnp.bfloat16)
    cond_mean = jnp.einsum(
        "sbjd,bjde->sbe", near_data, near_coef, preferred_element_type=jnp.float32
    )
    cond_mean = cond_mean + jnp.einsum(
        "sbjd,bjde->sbe", far_data, far_coef, preferred_element_type=jnp.float32
    )
    residual = (block_data.astype(jnp.float32) - cond_mean).astype(jnp.bfloat16)
    whitened = jnp.einsum(
        "sbd,bde->sbe", residual, inv_factor, preferred_element_type=jnp.float32
    ).astype(jnp.bfloat16)
    whitened = whitened.reshape(total_rows, blocks_here * block_width)
    return lax.all_to_all(whitened, "shard", split_axis=0, concat_axis=1, tiled=True)


def solution(mesh):
    return jax.shard_map(
        body,
        mesh=mesh,
        in_specs=(
            P("shard", "region"),
            P(("region", "shard"), None, None, None),
            P(("region", "shard"), None, None, None),
            P(("region", "shard"), None, None),
            P(("region", "shard"), None),
            P(("region", "shard"), None),
            P(("region", "shard"), None),
        ),
        out_specs=P("shard", "region"),
        check_vma=False,
    )
```

profile of v0, /device:TPU:0, one launch (start us, length us, event | category | flops | bytes accessed | tf_op | source)
XLA Modules:
  0.0 177.2 jit_solution(17149873583715637292)
XLA Ops:
  0.0 0.0 copy-start
  0.0 0.0 copy-start.4
  0.0 0.0 copy-start.2
  0.0 70.1 %all-gather = s32[32,4,2]{1,2,0:T(2,128)S(1)} all-gather(s32[1,4,2]{1,2,0:T(2,128)} %bitcast.97), channel_id=1, replica_groups=mesh['region'=4,'shard'=8] {'region','shard'}, dimensions={0}, use_global_device_ids=true | all-gather | bytes 1056 | tf_op jit(solution)/shard_map/all_gather | solution.py:39
  70.1 0.1 copy.72
  70.2 0.1 reshape.57
  70.3 0.1 copy.74
  70.4 0.1 copy.73
  70.5 63.7 %all-gather.1 = s32[32,4,2]{1,2,0:T(2,128)S(1)} all-gather(s32[1,4,2]{1,2,0:T(2,128)} %bitcast.98), channel_id=1, replica_groups=mesh['region'=4,'shard'=8] {'region','shard'}, dimensions={0}, use_global_device_ids=true | all-gather | bytes 1056 | tf_op jit(solution)/shard_map/all_gather | solution.py:40
  134.2 0.1 copy.76
  134.3 0.1 broadcast_in_dim.10
  134.4 0.1 copy.77
  134.4 0.7 convert_reduce_fusion
  135.1 0.2 select_reduce_fusion
  135.4 0.1 copy.78
  135.4 0.8 reshape.58
  136.2 0.2 fusion.1
  136.4 0.5 copy.92
  137.0 1.7 reshape.75
  138.7 3.3 %all-to-all-start = ((bf16[4,2,4096]{2,1,0:T(2,128)(2,1)}), bf16[4,2,4096]{2,1,0:T(2,128)(2,1)S(1)}, u32[]{:S(2)}, u32[]{:S(2)}) async-start(bf16[4,2,4096]{2,1,0:T(2,128)(2,1)} %reshape.75), calls=%async_computation | async-start | bytes 131072 | tf_op jit(solution)/shard_map/all_to_all | solution.py:55
  142.0 0.0 copy-done.4
  142.0 0.1 copy.85
  142.1 0.1 reshape.60
  142.2 0.2 convert_reduce_fusion.1
  142.4 0.0 copy-done.2
  142.4 0.3 copy.81
  142.7 3.4 %all-to-all-done = bf16[4,2,4096]{2,1,0:T(2,128)(2,1)S(1)} async-done(((bf16[4,2,4096]{2,1,0:T(2,128)(2,1)}), bf16[4,2,4096]{2,1,0:T(2,128)(2,1)S(1)}, u32[]{:S(2)}, u32[]{:S(2)}) %all-to-all-start) | async-done | bytes 65568 | tf_op jit(solution)/shard_map/all_to_all | solution.py:55
  146.1 1.2 reshape.76
  147.3 6.6 %pad_maximum_fusion = bf16[4,8,1536]{1,0,2:T(4,128)(2,1)S(1)} fusion(bf16[4,8,1024]{1,0,2:T(4,128)(2,1)S(1)} %bitcast.86, bf16[4,8,512]{1,0,2:T(4,128)(2,1)S(1)} %copy.81), kind=kLoop, calls=%fused_computation | loop fusion | flops 49152 | bytes 196608 | tf_op jit(solution)/shard_map/concatenate | solution.py:56
  153.9 0.0 copy-start.5
  153.9 0.0 copy-start.1
  153.9 0.0 copy-start.3
  153.9 1.8 %copy.82 = bf16[4,8,1536]{2,0,1:T(4,128)(2,1)} copy(bf16[4,8,1536]{1,0,2:T(4,128)(2,1)S(1)} %pad_maximum_fusion) | data formatting | bytes 196608 | tf_op jit(solution)/shard_map/concatenate | solution.py:56
  155.7 3.5 %all-to-all-start.1 = ((bf16[4,8,1536]{2,0,1:T(4,128)(2,1)}), bf16[4,8,1536]{2,0,1:T(4,128)(2,1)S(1)}, u32[]{:S(2)}, u32[]{:S(2)}) async-start(bf16[4,8,1536]{2,0,1:T(4,128)(2,1)} %copy.82), calls=%async_computation.1 | async-start | bytes 196608 | tf_op jit(solution)/shard_map/all_to_all | solution.py:59
  159.2 7.1 %all-to-all-done.1 = bf16[4,8,1536]{2,0,1:T(4,128)(2,1)S(1)} async-done(((bf16[4,8,1536]{2,0,1:T(4,128)(2,1)}), bf16[4,8,1536]{2,0,1:T(4,128)(2,1)S(1)}, u32[]{:S(2)}, u32[]{:S(2)}) %all-to-all-start.1) | async-done | bytes 98336 | tf_op jit(solution)/shard_map/all_to_all | solution.py:59
  166.5 0.2 convolution_convert_fusion.1
  166.7 0.0 copy-done.5
  166.7 0.2 fusion
  166.9 0.0 copy-done
  166.9 0.2 convolution_bitcast_fusion.1
  167.1 0.0 copy-done.1
  167.1 0.0 copy-done.3
  167.1 0.3 fusion.6
  167.5 9.1 %all_to_all.42 = bf16[8,4,512]{2,1,0:T(4,128)(2,1)S(1)} all-to-all(bf16[8,4,512]{2,1,0:T(4,128)(2,1)S(1)} %all_to_all.35), channel_id=1, replica_groups=mesh['region'=4,'shard'=8] {'shard'}, dimensions={0} | all-to-all | bytes 65536 | tf_op jit(solution)/shard_map/all_to_all | solution.py:87
  176.5 0.6 copy.109
  (12 shorter events, 0.2 us)
Async XLA Ops:
  0.0 166.9 %copy-start = (bf16[4,3,128,128]{3,2,1,0:T(8,128)(2,1)S(1)}, bf16[4,3,128,128]{3,2,1,0:T(8,128)(2,1)}, u32[]{:S(2)}) copy-start(bf16[4,3,128,128]{3,2,1,0:T(8,128)(2,1)} %param.8) | copy-start | bytes 1179652
  0.0 142.0 %copy-start.4 = (s32[4,2]{0,1:T(2,128)S(1)}, s32[4,2]{0,1:T(2,128)}, u32[]{:S(2)}) copy-start(s32[4,2]{0,1:T(2,128)} %param.12) | copy-start | bytes 100
  0.0 142.4 %copy-start.2 = (bf16[4,4096]{1,0:T(4,128)(2,1)S(1)}, bf16[4,4096]{1,0:T(4,128)(2,1)}, u32[]{:S(2)}) copy-start(bf16[4,4096]{1,0:T(4,128)(2,1)} %param.7) | copy-start | bytes 98308
  138.7 7.4 %all-to-all-start = ((bf16[4,2,4096]{2,1,0:T(2,128)(2,1)}), bf16[4,2,4096]{2,1,0:T(2,128)(2,1)S(1)}, u32[]{:S(2)}, u32[]{:S(2)}) async-start(bf16[4,2,4096]{2,1,0:T(2,128)(2,1)} %reshape.75), calls=%async_computation | async-start | bytes 131072 | tf_op jit(solution)/shard_map/all_to_all | solution.py:55
  153.9 12.8 %copy-start.5 = (s32[4,3]{1,0:T(4,128)S(1)}, s32[4,3]{1,0:T(4,128)}, u32[]{:S(2)}) copy-start(s32[4,3]{1,0:T(4,128)} %param.11) | copy-start | bytes 148
  153.9 13.2 %copy-start.1 = (bf16[4,2,128,128]{3,2,1,0:T(8,128)(2,1)S(1)}, bf16[4,2,128,128]{3,2,1,0:T(8,128)(2,1)}, u32[]{:S(2)}) copy-start(bf16[4,2,128,128]{3,2,1,0:T(8,128)(2,1)} %param.9) | copy-start | bytes 786436
  153.9 13.2 %copy-start.3 = (bf16[4,128,128]{2,1,0:T(8,128)(2,1)S(1)}, bf16[4,128,128]{2,1,0:T(8,128)(2,1)}, u32[]{:S(2)}) copy-start(bf16[4,128,128]{2,1,0:T(8,128)(2,1)} %param.10) | copy-start | bytes 393220
  155.7 10.6 %all-to-all-start.1 = ((bf16[4,8,1536]{2,0,1:T(4,128)(2,1)}), bf16[4,8,1536]{2,0,1:T(4,128)(2,1)S(1)}, u32[]{:S(2)}, u32[]{:S(2)}) async-start(bf16[4,8,1536]{2,0,1:T(4,128)(2,1)} %copy.82), calls=%async_computation.1 | async-start | bytes 196608 | tf_op jit(solution)/shard_map/all_to_all | solution.py:59
where the time goes:
time: 178 us; the launch traced here: 177 us
  blocking collectives  143 us (80%)
  waiting for transfers between devices  10.5 us (6%)
  local copies, waits for them, and re-layouts  8.01 us (4%)
  other arithmetic  7.7 us (4%)
  starting transfers between devices  6.77 us (4%)
    all_gather x1, blocking collectives, body(): lax.all_gather(far_region, ('region', 'shard'), axis=0, tiled=True)  70.1 us
    all_gather x1, blocking collectives, body(): lax.all_gather(far_block, ('region', 'shard'), axis=0, tiled=True)  63.7 us
    all_to_all x1, blocking collectives, body(): lax.all_to_all(whitened, 'shard', split_axis=0, concat_axis=1, tiled=True)  9.06 us
    all_to_all x1, waiting for transfers between devices, body(): lax.all_to_all(combined, 'shard', split_axis=1, concat_axis=0, tiled=True)  7.12 us
    concatenate x1, other arithmetic, body(): jnp.concatenate([fields.reshape(samp_rows, shard_count, blocks_here * blo...  6.58 us
    unnamed x19, local copies, waits for them, and re-layouts  3.67 us
  transfers between devices with their start and end apart: 2, of which 2 were waited for; matrix products, arithmetic and copies ran while one was open for 0% of the time, Pallas kernels for 0%

commit v1 on v0

v1 whole, which is shorter than its diff:
```python
import functools

import jax
import jax.numpy as jnp
from jax import lax
from jax.experimental import pallas as pl
from jax.experimental.pallas import tpu as pltpu
from jax.sharding import PartitionSpec as P

MESH = pl.DeviceIdType.MESH


def kernel(regions, shards, fields, near_coef, far_coef, inv_factor, near_block,
           far_region, far_block, out, own, near_land, far_land, near_x, near_w, far_w, inv_w, stage,
           load_sem, send_sem, recv_sem):
    rows = fields.shape[1]
    blocks, near, width = near_coef.shape[0], near_coef.shape[1], near_coef.shape[3]
    far = far_coef.shape[1]
    members = rows * shards
    r, s = lax.axis_index("region"), lax.axis_index("shard")

    def peer(dr, ds):
        return lax.rem(r + dr, regions), lax.rem(s + ds, shards)

    def each_shard(first, visit):
        if shards <= 8:
            for ds in range(first, shards):
                visit(ds)
        else:
            lax.fori_loop(first, shards, lambda ds, c: (visit(ds), c)[1], 0)

    barrier = pltpu.get_barrier_semaphore()
    for dr in range(regions):
        each_shard(1 if dr == 0 else 0, lambda ds: pl.semaphore_signal(
            barrier, inc=1, device_id=peer(dr, ds), device_id_type=MESH))

    loads = [pltpu.make_async_copy(a, b, load_sem.at[i]) for i, (a, b) in enumerate(
        [(fields, own), (near_coef, near_w), (far_coef, far_w), (inv_factor, inv_w)])]
    for load in loads:
        load.start()
    loads[0].wait()
    pl.semaphore_wait(barrier, regions * shards - 1)

    def group(index):
        return pl.ds(index * blocks, blocks)

    pltpu.make_async_copy(own.at[group(s)], near_land.at[:, s], recv_sem.at[0]).start()
    for dr in range(regions):
        stage_id = 0 if dr == 0 else 1
        place = far_land.at[group(regions - dr), s] if dr else near_land.at[:, s]

        def send(ds):
            rd, sd = peer(dr, ds)
            pltpu.make_async_remote_copy(
                src_ref=own.at[group(sd)], dst_ref=place,
                send_sem=send_sem.at[stage_id], recv_sem=recv_sem.at[stage_id],
                device_id=(rd, sd), device_id_type=MESH).start()

        each_shard(1 if dr == 0 else 0, send)

    def wait_for(ref, sem):
        pltpu.make_async_copy(ref, ref, sem).wait()

    wait_for(near_land, recv_sem.at[0])
    near_x[...] = near_land[...].reshape(blocks, members, width)
    far_land[:blocks] = near_land[...]
    loads[1].wait()
    means = []
    for b in range(blocks):
        x = jnp.concatenate([near_x[near_block[b, j]] for j in range(near)], axis=1)
        means.append(jnp.dot(x, near_w[b].reshape(near * width, width),
                             preferred_element_type=jnp.float32))
    loads[2].wait()
    loads[3].wait()
    others = far_land.at[pl.ds(blocks, (regions - 1) * blocks)]
    wait_for(others, recv_sem.at[1])
    for b in range(blocks):
        x = jnp.concatenate(
            [far_land[lax.rem(far_region[b, j] - r + regions, regions) * blocks
                      + far_block[b, j]].reshape(members, width) for j in range(far)], axis=1)
        mean = means[b] + jnp.dot(x, far_w[b].reshape(far * width, width),
                                  preferred_element_type=jnp.float32)
        residual = (near_x[b].astype(jnp.float32) - mean).astype(jnp.bfloat16)
        white = jnp.dot(residual, inv_w[b], preferred_element_type=jnp.float32)
        stage[:, b] = white.astype(jnp.bfloat16).reshape(shards, rows, width)

    pltpu.make_async_copy(stage.at[s], out.at[group(s)], recv_sem.at[2]).start()

    def give_back(ds):
        rd, sd = peer(0, ds)
        pltpu.make_async_remote_copy(
            src_ref=stage.at[sd], dst_ref=out.at[group(s)],
            send_sem=send_sem.at[2], recv_sem=recv_sem.at[2],
            device_id=(rd, sd), device_id_type=MESH).start()

    each_shard(1, give_back)
    wait_for(near_land.at[:, pl.ds(0, shards - 1)], send_sem.at[0])
    wait_for(others, send_sem.at[1])
    wait_for(stage.at[pl.ds(0, shards - 1)], send_sem.at[2])
    wait_for(out, recv_sem.at[2])


def body(fields, near_coef, far_coef, inv_factor, near_block, far_region, far_block):
    shards, regions = lax.axis_size("shard"), lax.axis_size("region")
    rows, columns = fields.shape
    blocks, width = near_coef.shape[0], near_coef.shape[3]
    tiles = columns // width
    tiled = jnp.transpose(fields.reshape(rows, tiles, width), (1, 0, 2))
    hbm = pl.BlockSpec(memory_space=pl.ANY)
    smem = pl.BlockSpec(memory_space=pltpu.SMEM)
    white = pl.pallas_call(
        functools.partial(kernel, regions, shards),
        out_shape=jax.ShapeDtypeStruct(tiled.shape, jnp.bfloat16),
        in_specs=[hbm] * 4 + [smem] * 3,
        out_specs=pl.BlockSpec(memory_space=pltpu.VMEM),
        scratch_shapes=[
            pltpu.VMEM(tiled.shape, jnp.bfloat16),
            pltpu.VMEM((blocks, shards, rows, width), jnp.bfloat16),
            pltpu.VMEM((regions * blocks, shards, rows, width), jnp.bfloat16),
            pltpu.VMEM((blocks, shards * rows, width), jnp.bfloat16),
            pltpu.VMEM(near_coef.shape, jnp.bfloat16),
            pltpu.VMEM(far_coef.shape, jnp.bfloat16),
            pltpu.VMEM(inv_factor.shape, jnp.bfloat16),
            pltpu.VMEM((shards, blocks, rows, width), jnp.bfloat16),
            pltpu.SemaphoreType.DMA((4,)),
            pltpu.SemaphoreType.DMA((3,)),
            pltpu.SemaphoreType.DMA((3,)),
        ],
        compiler_params=pltpu.CompilerParams(collective_id=0, has_side_effects=True),
    )(tiled, near_coef, far_coef, inv_factor, near_block, far_region, far_block)
    return jnp.transpose(white, (1, 0, 2)).reshape(rows, columns)


def solution(mesh):
    return jax.shard_map(
        body,
        mesh=mesh,
        in_specs=(
            P("shard", "region"),
            P(("region", "shard"), None, None, None),
            P(("region", "shard"), None, None, None),
            P(("region", "shard"), None, None),
            P(("region", "shard"), None),
            P(("region", "shard"), None),
            P(("region", "shard"), None),
        ),
        out_specs=P("shard", "region"),
        check_vma=False,
    )
```

time: 178 us -> 22 us (0.12)
  blocking collectives: 143 us -> 0 us
  Pallas kernels: 0 us -> 18.4 us
  waiting for transfers between devices: 10.5 us -> 0 us
  other arithmetic: 7.7 us -> 0 us
  starting transfers between devices: 6.77 us -> 0 us
  local copies, waits for them, and re-layouts: 8.01 us -> 3.39 us
    all_gather x2 -> x0, blocking collectives: 134 us -> none  [the longest x1 70.1 us: body(): lax.all_gather(far_region, ('region', 'shard'), axis=0, tiled=True)]
    pallas_call x0 -> x1, Pallas kernels: none -> 18.4 us  [body(): pl.pallas_call(functools.partial(kernel, regions, shards), out_shape=jax....]
    all_to_all x2 -> x0, waiting for transfers between devices: 10.5 us -> none  [the longest x1 7.12 us: body(): lax.all_to_all(combined, 'shard', split_axis=1, concat_axis=0, tiled=True)]
    all_to_all x1 -> x0, blocking collectives: 9.06 us -> none  [body(): lax.all_to_all(whitened, 'shard', split_axis=0, concat_axis=1, tiled=True)]
    all_to_all x2 -> x0, starting transfers between devices: 6.77 us -> none  [the longest x1 3.49 us: body(): lax.all_to_all(combined, 'shard', split_axis=1, concat_axis=0, tiled=True)]
    concatenate x1 -> x0, other arithmetic: 6.58 us -> none  [body(): jnp.concatenate([fields.reshape(samp_rows, shard_count, blocks_here * blo...]
    reshape x6 -> x0, local copies, waits for them, and re-layouts: 1.92 us -> none  [the longest x1 0.81 us: body(): fields.reshape(samp_rows, shard_count, blocks_here, block_width)]
    concatenate x1 -> x0, local copies, waits for them, and re-layouts: 1.81 us -> none  [body(): jnp.concatenate([fields.reshape(samp_rows, shard_count, blocks_here * blo...]
  transfers between devices with their start and end apart: 2 -> 0, of which waited for: 2 -> 0; matrix products, arithmetic and copies ran while one was open for 0% -> 0% of each run, Pallas kernels for 0% -> 0%
where the time goes in v1:
time: 22 us; the launch traced here: 21.8 us
  Pallas kernels  18.4 us (84%)
  local copies, waits for them, and re-layouts  3.39 us (15%)
    pallas_call x1, Pallas kernels, body(): pl.pallas_call(functools.partial(kernel, regions, shards), out_shape=jax....  18.4 us
    unnamed x7, local copies, waits for them, and re-layouts  3.39 us

profile of v1, /device:TPU:0, one launch (start us, length us, event | category | flops | bytes accessed | tf_op | source)
XLA Modules:
  0.0 21.8 jit_solution(1895518591327209601)
XLA Ops:
  0.0 0.0 copy-start
  0.0 0.7 %copy-done = s32[4,2]{0,1:T(2,128)S(1)} copy-done((s32[4,2]{0,1:T(2,128)S(1)}, s32[4,2]{0,1:T(2,128)}, u32[]{:S(2)}) %copy-start) | copy-done | bytes 56
  0.7 0.0 copy-start.1
  0.7 0.7 %copy.8.far_region = s32[4,2]{1,0:T(4,128)} copy(s32[4,2]{0,1:T(2,128)S(1)} %copy-done) | data formatting | bytes 64 | tf_op args[5]
  1.3 0.0 copy-done.1
  1.4 0.6 %copy.9.far_block = s32[4,2]{1,0:T(4,128)} copy(s32[4,2]{0,1:T(2,128)S(1)} %copy-done.1) | data formatting | bytes 64 | tf_op args[6]
  2.0 18.4 %shard_map.73 = bf16[32,4,128]{2,1,0:T(4,128)(2,1)} custom-call(bf16[32,4,128]{2,1,0:T(4,128)(2,1)} %bitcast.7, bf16[4,3,128,128]{3,2,1,0:T(8,128)(2,1)} %near_coef.1, bf16[4,2,128,128]{3,2,1,0:T(8,128)(2,1)} %far_coef.1, bf16[4,128,128]{2,1,0:T(8,128)(2,1)} %inv_factor.1, s32[4,3]{1,0:T(4,128)} %near_block.1, s32[4,2]{1,0:T(4,128)} %copy.8.far_region, ...), custom_call_target="tpu_custom_call" | custom-call | tf_op jit(solution)/shard_map/pallas_call | solution.py:111
  20.4 1.4 %copy.11 = bf16[4,4096]{1,0:T(4,128)(2,1)} copy(bf16[4,4096]{1,0:T(4,128)(2,1)} %bitcast.6) | data formatting | bytes 65536
Async XLA Ops:
  0.0 0.7 %copy-start = (s32[4,2]{0,1:T(2,128)S(1)}, s32[4,2]{0,1:T(2,128)}, u32[]{:S(2)}) copy-start(s32[4,2]{0,1:T(2,128)} %param.12) | copy-start | bytes 100
  0.7 0.7 %copy-start.1 = (s32[4,2]{0,1:T(2,128)S(1)}, s32[4,2]{0,1:T(2,128)}, u32[]{:S(2)}) copy-start(s32[4,2]{0,1:T(2,128)} %param.13) | copy-start | bytes 100

commit v2 on v1

--- a/solution.py
+++ b/solution.py
@@ -10,9 +10,9 @@
 MESH = pl.DeviceIdType.MESH
 
 
-def kernel(regions, shards, fields, near_coef, far_coef, inv_factor, near_block,
-           far_region, far_block, out, own, near_land, far_land, near_x, near_w, far_w, inv_w, stage,
-           load_sem, send_sem, recv_sem):
+def kernel(regions, shards, fields, near_coef, far_coef, inv_factor, near_list,
+           region_list, block_list, out, own, near_land, far_land, near_x, near_w,
+           far_w, inv_w, stage, near_block, far_region, far_block, load_sem, send_sem, recv_sem):
     rows = fields.shape[1]
     blocks, near, width = near_coef.shape[0], near_coef.shape[1], near_coef.shape[3]
     far = far_coef.shape[1]
@@ -30,54 +30,64 @@
             lax.fori_loop(first, shards, lambda ds, c: (visit(ds), c)[1], 0)
 
     barrier = pltpu.get_barrier_semaphore()
-    for dr in range(regions):
-        each_shard(1 if dr == 0 else 0, lambda ds: pl.semaphore_signal(
-            barrier, inc=1, device_id=peer(dr, ds), device_id_type=MESH))
+
+    def greet(dr, ds):
+        pl.semaphore_signal(barrier, inc=1, device_id=peer(dr, ds), device_id_type=MESH)
+
+    each_shard(1, lambda ds: greet(0, ds))
+    for dr in range(1, regions):
+        greet(dr, 0)
 
     loads = [pltpu.make_async_copy(a, b, load_sem.at[i]) for i, (a, b) in enumerate(
-        [(fields, own), (near_coef, near_w), (far_coef, far_w), (inv_factor, inv_w)])]
+        [(fields, own), (near_list, near_block), (region_list, far_region),
+         (block_list, far_block), (near_coef, near_w), (far_coef, far_w),
+         (inv_factor, inv_w)])]
     for load in loads:
         load.start()
     loads[0].wait()
-    pl.semaphore_wait(barrier, regions * shards - 1)
+    pl.semaphore_wait(barrier, shards + regions - 2)
 
     def group(index):
         return pl.ds(index * blocks, blocks)
 
     pltpu.make_async_copy(own.at[group(s)], near_land.at[:, s], recv_sem.at[0]).start()
-    for dr in range(regions):
-        stage_id = 0 if dr == 0 else 1
-        place = far_land.at[group(regions - dr), s] if dr else near_land.at[:, s]
 
-        def send(ds):
-            rd, sd = peer(dr, ds)
-            pltpu.make_async_remote_copy(
-                src_ref=own.at[group(sd)], dst_ref=place,
-                send_sem=send_sem.at[stage_id], recv_sem=recv_sem.at[stage_id],
-                device_id=(rd, sd), device_id_type=MESH).start()
+    def gather(ds):
+        rd, sd = peer(0, ds)
+        pltpu.make_async_remote_copy(
+            src_ref=own.at[group(sd)], dst_ref=near_land.at[:, s],
+            send_sem=send_sem.at[0], recv_sem=recv_sem.at[0],
+            device_id=(rd, sd), device_id_type=MESH).start()
 
-        each_shard(1 if dr == 0 else 0, send)
+    each_shard(1, gather)
 
     def wait_for(ref, sem):
         pltpu.make_async_copy(ref, ref, sem).wait()
 
     wait_for(near_land, recv_sem.at[0])
+    for dr in range(1, regions):
+        rd, sd = peer(dr, 0)
+        pltpu.make_async_remote_copy(
+            src_ref=near_land, dst_ref=far_land.at[group(regions - dr)],
+            send_sem=send_sem.at[1], recv_sem=recv_sem.at[1],
+            device_id=(rd, sd), device_id_type=MESH).start()
     near_x[...] = near_land[...].reshape(blocks, members, width)
     far_land[:blocks] = near_land[...]
-    loads[1].wait()
+    for load in loads[1:5]:
+        load.wait()
     means = []
     for b in range(blocks):
         x = jnp.concatenate([near_x[near_block[b, j]] for j in range(near)], axis=1)
         means.append(jnp.dot(x, near_w[b].reshape(near * width, width),
                              preferred_element_type=jnp.float32))
-    loads[2].wait()
-    loads[3].wait()
+    loads[5].wait()
+    loads[6].wait()
     others = far_land.at[pl.ds(blocks, (regions - 1) * blocks)]
     wait_for(others, recv_sem.at[1])
     for b in range(blocks):
         x = jnp.concatenate(
-            [far_land[lax.rem(far_region[b, j] - r + regions, regions) * blocks
-                      + far_block[b, j]].reshape(members, width) for j in range(far)], axis=1)
+            [far_land[lax.rem(far_region[j, b] - r + regions, regions) * blocks
+                      + far_block[j, b]].reshape(members, width) for j in range(far)], axis=1)
         mean = means[b] + jnp.dot(x, far_w[b].reshape(far * width, width),
                                   preferred_element_type=jnp.float32)
         residual = (near_x[b].astype(jnp.float32) - mean).astype(jnp.bfloat16)
@@ -107,11 +117,10 @@
     tiles = columns // width
     tiled = jnp.transpose(fields.reshape(rows, tiles, width), (1, 0, 2))
     hbm = pl.BlockSpec(memory_space=pl.ANY)
-    smem = pl.BlockSpec(memory_space=pltpu.SMEM)
     white = pl.pallas_call(
         functools.partial(kernel, regions, shards),
-        out_shape=jax.ShapeDtypeStruct(tiled.shape, jnp.bfloat16),
-        in_specs=[hbm] * 4 + [smem] * 3,
+        out_shape=pltpu.VMEM(tiled.shape, jnp.bfloat16),
+        in_specs=[hbm] * 7,
         out_specs=pl.BlockSpec(memory_space=pltpu.VMEM),
         scratch_shapes=[
             pltpu.VMEM(tiled.shape, jnp.bfloat16),
@@ -122,12 +131,15 @@
             pltpu.VMEM(far_coef.shape, jnp.bfloat16),
             pltpu.VMEM(inv_factor.shape, jnp.bfloat16),
             pltpu.VMEM((shards, blocks, rows, width), jnp.bfloat16),
-            pltpu.SemaphoreType.DMA((4,)),
+            pltpu.SMEM(near_block.shape, jnp.int32),
+            pltpu.SMEM(far_region.T.shape, jnp.int32),
+            pltpu.SMEM(far_block.T.shape, jnp.int32),
+            pltpu.SemaphoreType.DMA((7,)),
             pltpu.SemaphoreType.DMA((3,)),
             pltpu.SemaphoreType.DMA((3,)),
         ],
         compiler_params=pltpu.CompilerParams(collective_id=0, has_side_effects=True),
-    )(tiled, near_coef, far_coef, inv_factor, near_block, far_region, far_block)
+    )(tiled, near_coef, far_coef, inv_factor, near_block, far_region.T, far_block.T)
     return jnp.transpose(white, (1, 0, 2)).reshape(rows, columns)
 
 

time: 22 us -> 19.1 us (0.87)
  local copies, waits for them, and re-layouts: 3.39 us -> 0.62 us
    unnamed x7 -> x1, local copies, waits for them, and re-layouts: 3.39 us -> 0.62 us
where the time goes in v2:
time: 19.1 us; the launch traced here: 18.9 us
  Pallas kernels  18.3 us (96%)
  local copies, waits for them, and re-layouts  0.62 us (3%)
    pallas_call x1, Pallas kernels, body(): pl.pallas_call(functools.partial(kernel, regions, shards), out_shape=pltp...  18.3 us
    unnamed x1, local copies, waits for them, and re-layouts  0.62 us

profile of v2, /device:TPU:0, one launch (start us, length us, event | category | flops | bytes accessed | tf_op | source)
XLA Modules:
  0.0 18.9 jit_solution(16981037642980971521)
XLA Ops:
  0.0 18.3 %shard_map.73 = bf16[32,4,128]{2,1,0:T(4,128)(2,1)S(1)} custom-call(bf16[32,4,128]{2,1,0:T(4,128)(2,1)} %bitcast.9, bf16[4,3,128,128]{3,2,1,0:T(8,128)(2,1)} %near_coef.1, bf16[4,2,128,128]{3,2,1,0:T(8,128)(2,1)} %far_coef.1, bf16[4,128,128]{2,1,0:T(8,128)(2,1)} %inv_factor.1, s32[4,3]{1,0:T(4,128)} %near_list.1, s32[2,4]{1,0:T(2,128)} %bitcast.10, ...), custom_call_target="tpu_custom_call" | custom-call | tf_op jit(solution)/shard_map/pallas_call | solution.py:120
  18.3 0.6 %copy.9 = bf16[4,4096]{1,0:T(4,128)(2,1)} copy(bf16[4,4096]{1,0:T(4,128)(2,1)S(1)} %bitcast.8) | data formatting | bytes 65536

commit v3 on v2

--- a/solution.py
+++ b/solution.py
@@ -7,12 +7,14 @@
 from jax.experimental.pallas import tpu as pltpu
 from jax.sharding import PartitionSpec as P
 
+WAVES = 4
+DIRECT = (1, 2, 3)
 MESH = pl.DeviceIdType.MESH
 
 
 def kernel(regions, shards, fields, near_coef, far_coef, inv_factor, near_list,
            region_list, block_list, out, own, near_land, far_land, near_x, near_w,
-           far_w, inv_w, stage, near_block, far_region, far_block, load_sem, send_sem, recv_sem):
+           far_w, inv_w, stage, near_block, far_region, far_block, load_sem, send_sem, recv_sem, near_sem):
     rows = fields.shape[1]
     blocks, near, width = near_coef.shape[0], near_coef.shape[1], near_coef.shape[3]
     far = far_coef.shape[1]
@@ -22,21 +24,29 @@
     def peer(dr, ds):
         return lax.rem(r + dr, regions), lax.rem(s + ds, shards)
 
-    def each_shard(first, visit):
-        if shards <= 8:
-            for ds in range(first, shards):
-                visit(ds)
-        else:
-            lax.fori_loop(first, shards, lambda ds, c: (visit(ds), c)[1], 0)
+    run = shards // WAVES
+
+    def flipped(q, w):
+        for bit in (1, 2):
+            if w & bit:
+                q = q + bit * (1 - 2 * lax.rem(lax.div(q, bit), 2))
+        return q
+
+    mine = lax.div(s, run)
+
+    def partner(w, i):
+        return flipped(mine, w) * run + lax.rem(lax.rem(s, run) + i, run)
 
     barrier = pltpu.get_barrier_semaphore()
-
-    def greet(dr, ds):
-        pl.semaphore_signal(barrier, inc=1, device_id=peer(dr, ds), device_id_type=MESH)
-
-    each_shard(1, lambda ds: greet(0, ds))
-    for dr in range(1, regions):
-        greet(dr, 0)
+    met = 0
+    for w in range(WAVES):
+        for i in range(run):
+            for dr in range(regions):
+                if (w or i) if dr == 0 else (w in DIRECT or (w == 0 and i == 0)):
+                    met += 1
+                    pl.semaphore_signal(
+                        barrier, inc=1, device_id=(lax.rem(r + dr, regions), partner(w, i)),
+                        device_id_type=MESH)
 
     loads = [pltpu.make_async_copy(a, b, load_sem.at[i]) for i, (a, b) in enumerate(
         [(fields, own), (near_list, near_block), (region_list, far_region),
@@ -45,32 +55,41 @@
     for load in loads:
         load.start()
     loads[0].wait()
-    pl.semaphore_wait(barrier, shards + regions - 2)
+    pl.semaphore_wait(barrier, met)
 
     def group(index):
         return pl.ds(index * blocks, blocks)
 
-    pltpu.make_async_copy(own.at[group(s)], near_land.at[:, s], recv_sem.at[0]).start()
+    def visit(w, i, dr):
+        sd = partner(w, i)
+        pltpu.make_async_remote_copy(
+            src_ref=own.at[group(sd)],
+            dst_ref=far_land.at[group(regions - dr), s] if dr else near_land.at[:, s],
+            send_sem=send_sem.at[1 if dr else 0],
+            recv_sem=recv_sem.at[1] if dr else near_sem.at[w],
+            device_id=(lax.rem(r + dr, regions), sd), device_id_type=MESH).start()
 
-    def gather(ds):
-        rd, sd = peer(0, ds)
-        pltpu.make_async_remote_copy(
-            src_ref=own.at[group(sd)], dst_ref=near_land.at[:, s],
-            send_sem=send_sem.at[0], recv_sem=recv_sem.at[0],
-            device_id=(rd, sd), device_id_type=MESH).start()
-
-    each_shard(1, gather)
+    pltpu.make_async_copy(own.at[group(s)], near_land.at[:, s], near_sem.at[0]).start()
+    for w in reversed(range(WAVES)):
+        for i in range(1 if w == 0 else 0, run):
+            visit(w, i, 0)
+    for w in reversed(DIRECT):
+        for i in range(run):
+            for dr in range(1, regions):
+                visit(w, i, dr)
 
     def wait_for(ref, sem):
         pltpu.make_async_copy(ref, ref, sem).wait()
 
-    wait_for(near_land, recv_sem.at[0])
-    for dr in range(1, regions):
-        rd, sd = peer(dr, 0)
-        pltpu.make_async_remote_copy(
-            src_ref=near_land, dst_ref=far_land.at[group(regions - dr)],
-            send_sem=send_sem.at[1], recv_sem=recv_sem.at[1],
-            device_id=(rd, sd), device_id_type=MESH).start()
+    for w in range(WAVES):
+        part = pl.ds(flipped(mine, w) * run, run)
+        wait_for(near_land.at[:, part], near_sem.at[w])
+        for dr in range(1, regions if w not in DIRECT else 1):
+            pltpu.make_async_remote_copy(
+                src_ref=near_land.at[:, part],
+                dst_ref=far_land.at[group(regions - dr), part],
+                send_sem=send_sem.at[1], recv_sem=recv_sem.at[1],
+                device_id=peer(dr, 0), device_id_type=MESH).start()
     near_x[...] = near_land[...].reshape(blocks, members, width)
     far_land[:blocks] = near_land[...]
     for load in loads[1:5]:
@@ -96,14 +115,16 @@
 
     pltpu.make_async_copy(stage.at[s], out.at[group(s)], recv_sem.at[2]).start()
 
-    def give_back(ds):
-        rd, sd = peer(0, ds)
+    def give_back(sd):
         pltpu.make_async_remote_copy(
             src_ref=stage.at[sd], dst_ref=out.at[group(s)],
             send_sem=send_sem.at[2], recv_sem=recv_sem.at[2],
-            device_id=(rd, sd), device_id_type=MESH).start()
+            device_id=(r, sd), device_id_type=MESH).start()
 
-    each_shard(1, give_back)
+    for w in reversed(range(WAVES)):
+        for i in range(1 if w == 0 else 0, run):
+            give_back(partner(w, i))
+
     wait_for(near_land.at[:, pl.ds(0, shards - 1)], send_sem.at[0])
     wait_for(others, send_sem.at[1])
     wait_for(stage.at[pl.ds(0, shards - 1)], send_sem.at[2])
@@ -137,6 +158,7 @@
             pltpu.SemaphoreType.DMA((7,)),
             pltpu.SemaphoreType.DMA((3,)),
             pltpu.SemaphoreType.DMA((3,)),
+            pltpu.SemaphoreType.DMA((WAVES,)),
         ],
         compiler_params=pltpu.CompilerParams(collective_id=0, has_side_effects=True),
     )(tiled, near_coef, far_coef, inv_factor, near_block, far_region.T, far_block.T)

time: 19.1 us -> 17.6 us (0.921)
  Pallas kernels: 18.3 us -> 16.8 us
    pallas_call x1, Pallas kernels: 18.3 us -> 16.8 us  [body(): pl.pallas_call(functools.partial(kernel, regions, shards), out_shape=pltp...]
where the time goes in v3:
time: 17.6 us; the launch traced here: 17.4 us
  Pallas kernels  16.8 us (95%)
  local copies, waits for them, and re-layouts  0.62 us (4%)
    pallas_call x1, Pallas kernels, body(): pl.pallas_call(functools.partial(kernel, regions, shards), out_shape=pltp...  16.8 us
    unnamed x1, local copies, waits for them, and re-layouts  0.62 us

profile of v3, /device:TPU:0, one launch (start us, length us, event | category | flops | bytes accessed | tf_op | source)
XLA Modules:
  0.0 17.4 jit_solution(16195300082233621642)
XLA Ops:
  0.0 16.8 %shard_map.73 = bf16[32,4,128]{2,1,0:T(4,128)(2,1)S(1)} custom-call(bf16[32,4,128]{2,1,0:T(4,128)(2,1)} %bitcast.9, bf16[4,3,128,128]{3,2,1,0:T(8,128)(2,1)} %near_coef.1, bf16[4,2,128,128]{3,2,1,0:T(8,128)(2,1)} %far_coef.1, bf16[4,128,128]{2,1,0:T(8,128)(2,1)} %inv_factor.1, s32[4,3]{1,0:T(4,128)} %near_list.1, s32[2,4]{1,0:T(2,128)} %bitcast.10, ...), custom_call_target="tpu_custom_call" | custom-call | tf_op jit(solution)/shard_map/pallas_call | solution.py:141
  16.8 0.6 %copy.9 = bf16[4,4096]{1,0:T(4,128)(2,1)} copy(bf16[4,4096]{1,0:T(4,128)(2,1)S(1)} %bitcast.8) | data formatting | bytes 65536

commit v4 on v3

--- a/solution.py
+++ b/solution.py
@@ -7,8 +7,8 @@
 from jax.experimental.pallas import tpu as pltpu
 from jax.sharding import PartitionSpec as P
 
-WAVES = 4
-DIRECT = (1, 2, 3)
+WAVES = 8
+DIRECT = (2, 3, 4, 5, 6, 7)
 MESH = pl.DeviceIdType.MESH
 
 
@@ -27,7 +27,7 @@
     run = shards // WAVES
 
     def flipped(q, w):
-        for bit in (1, 2):
+        for bit in (1, 2, 4):
             if w & bit:
                 q = q + bit * (1 - 2 * lax.rem(lax.div(q, bit), 2))
         return q

time: 17.6 us -> 17.3 us (0.983)
  Pallas kernels: 16.8 us -> 16.5 us
    pallas_call x1, Pallas kernels: 16.8 us -> 16.5 us  [body(): pl.pallas_call(functools.partial(kernel, regions, shards), out_shape=pltp...]
where the time goes in v4:
time: 17.3 us; the launch traced here: 17.2 us
  Pallas kernels  16.5 us (95%)
  local copies, waits for them, and re-layouts  0.62 us (4%)
    pallas_call x1, Pallas kernels, body(): pl.pallas_call(functools.partial(kernel, regions, shards), out_shape=pltp...  16.5 us
    unnamed x1, local copies, waits for them, and re-layouts  0.62 us

profile of v4, /device:TPU:0, one launch (start us, length us, event | category | flops | bytes accessed | tf_op | source)
XLA Modules:
  0.0 17.2 jit_solution(17531933154796996451)
XLA Ops:
  0.0 16.5 %shard_map.73 = bf16[32,4,128]{2,1,0:T(4,128)(2,1)S(1)} custom-call(bf16[32,4,128]{2,1,0:T(4,128)(2,1)} %bitcast.9, bf16[4,3,128,128]{3,2,1,0:T(8,128)(2,1)} %near_coef.1, bf16[4,2,128,128]{3,2,1,0:T(8,128)(2,1)} %far_coef.1, bf16[4,128,128]{2,1,0:T(8,128)(2,1)} %inv_factor.1, s32[4,3]{1,0:T(4,128)} %near_list.1, s32[2,4]{1,0:T(2,128)} %bitcast.10, ...), custom_call_target="tpu_custom_call" | custom-call | tf_op jit(solution)/shard_map/pallas_call | solution.py:141
  16.5 0.6 %copy.9 = bf16[4,4096]{1,0:T(4,128)(2,1)} copy(bf16[4,4096]{1,0:T(4,128)(2,1)S(1)} %bitcast.8) | data formatting | bytes 65536
